TPU v7x, 512 devices: a whole 4x8x8 slice. The times are simulated.
512 devices in a mesh: ev: 32 (over x, y_lo, core), ch: 16 (over y_hi, z).
Axes of the slice: x: 4, y: 8 (y_hi: 2, y_lo: 4; y = y_hi * 4 + y_lo), z: 8, core: 2. Of those that a mesh axis runs over, the one named last changes fastest.
Arguments:
- spectra: float32 [512, 16, 65536], P('ev', None, 'ch'), as said below
- tile_mask: int32 [512, 512], P('ev', 'ch'), may hold values 0 or 1
- source_init: float32 [512, 16], P('ev'), may hold values from -6 to 6
- site_init: float32 [16, 65536], P(None, 'ch'), may hold values from -6 to 6
- event_pos: float32 [3, 512], P(None, 'ev'), may hold values from 5 to 50
- channel_pos: float32 [2, 65536], P(None, 'ch'), may hold values from 0 to 50
- atten: float32 [16], replicated, may hold values from 0.02 to 0.3
Outputs:
- source: float32 [512, 16], P('ev')
- site: float32 [16, 65536], P(None, 'ch')
Inputs may be any that keep to these rules, and one draw needn't show every extreme that they name: spectra are log amplitudes of order one to a few, with outliers. `tile_mask`: 0 marks an event invalid on a whole tile of 128 channels.
All inputs are finite; a program needn't handle non-finite values. No bound on the sum of `tile_mask` on one device may be relied on, other than what follows from the above.
Results may differ from a plain program's by a relative error of at most 0.0001.
Values sent between devices are 32-bit elements; how exact they have to be, the bound alone decides.
A program may use at most 64 MiB of HBM per device.

v0:
```python
import jax
import jax.numpy as jnp
from jax import lax
from jax.sharding import PartitionSpec as P

ITERS = 2


def on_device(spectra, tile_mask, source_init, site_init, event_pos, channel_pos, atten):
    ev_n, freqs, ch_n = spectra.shape
    total_ch = ch_n * lax.axis_size("ch")
    valid = jnp.repeat(tile_mask, 128, axis=1).astype(jnp.float32)[:, None, :]
    count_part = jnp.sum(valid)
    east = event_pos[0][:, None] - channel_pos[0][None, :]
    north = event_pos[1][:, None] - channel_pos[1][None, :]
    depth = event_pos[2][:, None]
    travel = jnp.sqrt(east * east + north * north + depth * depth) / 3.0
    path = atten[None, :, None] * travel[:, None, :]
    source = source_init
    site = site_init
    for step in range(ITERS):
        resid = spectra - source[:, :, None] - site[None, :, :] + path
        abs_part = jnp.sum(valid * jnp.abs(resid), axis=(0, 2))
        absum, count = lax.psum((abs_part, count_part), ("ev", "ch"))
        delta = 1.345 * (1.2533 * absum / jnp.maximum(count, 1.0) + 1e-05)
        limit = delta[None, :, None]
        weight = limit / jnp.maximum(jnp.abs(resid), limit) * valid
        product = weight * resid
        src_num, src_den = lax.psum((jnp.sum(product, axis=2), jnp.sum(weight, axis=2)), "ch")
        site_num = jnp.sum(product, axis=0)
        site_den = jnp.sum(weight, axis=0)
        site_num, site_den = lax.psum((site_num, site_den), "ev")
        site = site + 0.5 * site_num / (site_den + 1.0)
        source = source + 0.5 * src_num / (src_den + 1.0)
        shift = lax.psum(jnp.sum(site, axis=1), "ch") / total_ch
        site = site - shift[:, None]
        source = source + shift[None, :]
    return (source, site)


def solution(mesh):
    in_specs = (
        P("ev", None, "ch"),
        P("ev", "ch"),
        P("ev", None),
        P(None, "ch"),
        P(None, "ev"),
        P(None, "ch"),
        P(),
    )
    out_specs = (P("ev", None), P(None, "ch"))
    return jax.shard_map(
        on_device, mesh=mesh, in_specs=in_specs, out_specs=out_specs, check_vma=False
    )
```

profile of v0, /device:TPU:8, one launch (start us, length us, event | category | flops | bytes accessed | tf_op | source)
XLA Modules:
  0.0 981.2 jit_solution(700504949465934503)
XLA Ops:
  7.2 0.0 copy-start.2
  7.2 0.0 copy-start
  7.2 0.0 copy-start.1
  7.2 0.0 all-reduce.10.cloned.1.call-start
  7.2 0.8 slice_bitcast_fusion.1
  8.0 0.7 convert_element_type.13
  8.7 0.9 fusion.8
  9.6 0.1 broadcast_in_dim.2
  9.7 0.2 copy.11
  9.9 0.2 sqrt_multiply_fusion
  10.1 3.4 multiply_reduce_fusion.1
  13.5 0.7 broadcast_reduce_fusion
  14.2 104.9 %all-reduce = (f32[16]{0:T(128)S(1)}, f32[]{:T(128)}) all-reduce(f32[16]{0:T(128)S(1)} %multiply_reduce_fusion.1, f32[]{:T(128)} %broadcast_reduce_fusion), channel_id=1, replica_groups=mesh['ev'=32,'ch'=16] {'ev','ch'}, use_global_device_ids=true, to_apply=%region_1.0 | all-reduce | flops 17 | bytes 136 | tf_op jit(solution)/shard_map/psum | solution.py:24
  119.7 0.0 copy-done.2
  119.8 0.0 copy-done
  119.8 0.0 copy-done.1
  119.8 5.4 fusion.4
  125.1 0.0 all-reduce.10.cloned.1.call-update
  125.2 0.0 all-reduce.8.cloned.1.call-start
  125.2 271.7 %all-reduce.10.cloned.1.call-done = (f32[16,4096]{1,0:T(8,128)}, f32[16,4096]{1,0:T(8,128)}) async-done(((f32[16,4096]{1,0:T(8,128)}, f32[16,4096]{1,0:T(8,128)}), (f32[16,4096]{1,0:T(8,128)}, f32[16,4096]{1,0:T(8,128)})) %all-reduce.10.cloned.1.call-update) | async-done | bytes 524304 | tf_op jit(solution)/shard_map/psum | solution.py:32
  397.0 1.2 fusion.7
  398.2 98.8 %all-reduce.4 = (f32[16,16]{1,0:T(8,128)S(1)}, f32[16,16]{1,0:T(8,128)S(1)}, f32[16]{0:T(128)S(1)}) all-reduce(f32[16,16]{1,0:T(8,128)S(1)} %get-tuple-element.9, f32[16,16]{1,0:T(8,128)S(1)} %get-tuple-element.5, f32[16]{0:T(128)S(1)} %get-tuple-element.24), channel_id=1, replica_groups=mesh['ev'=32,'ch'=16] {'ch'}, use_global_device_ids=true, to_apply=%region_7.0 | all-reduce | flops 528 | bytes 4224 | tf_op jit(solution)/shard_map/psum | solution.py:29
  497.0 0.1 broadcast_subtract_fusion.1
  497.1 3.3 multiply_reduce_fusion
  500.4 97.2 %psum.101 = f32[16]{0:T(128)S(1)} all-reduce(f32[16]{0:T(128)S(1)} %multiply_reduce_fusion), channel_id=1, replica_groups=mesh['ev'=32,'ch'=16] {'ev','ch'}, use_global_device_ids=true, to_apply=%region_15.0 | all-reduce | flops 16 | bytes 128 | tf_op jit(solution)/shard_map/psum | solution.py:24
  597.6 5.4 fusion.2
  602.9 0.0 all-reduce.8.cloned.1.call-update
  603.0 270.0 %all-reduce.8.cloned.1.call-done = (f32[16,4096]{1,0:T(8,128)}, f32[16,4096]{1,0:T(8,128)}) async-done(((f32[16,4096]{1,0:T(8,128)}, f32[16,4096]{1,0:T(8,128)}), (f32[16,4096]{1,0:T(8,128)}, f32[16,4096]{1,0:T(8,128)})) %all-reduce.8.cloned.1.call-update) | async-done | bytes 524304 | tf_op jit(solution)/shard_map/psum | solution.py:32
  872.9 1.2 fusion.6
  874.2 98.8 %all-reduce.3 = (f32[16,16]{1,0:T(8,128)S(1)}, f32[16,16]{1,0:T(8,128)S(1)}, f32[16]{0:T(128)S(1)}) all-reduce(f32[16,16]{1,0:T(8,128)S(1)} %get-tuple-element.7, f32[16,16]{1,0:T(8,128)S(1)} %get-tuple-element.3, f32[16]{0:T(128)S(1)} %get-tuple-element.22), channel_id=1, replica_groups=mesh['ev'=32,'ch'=16] {'ch'}, use_global_device_ids=true, to_apply=%region_19.0 | all-reduce | flops 528 | bytes 4224 | tf_op jit(solution)/shard_map/psum | solution.py:29
  973.0 0.8 broadcast_subtract_fusion
  973.8 0.6 add_add_fusion
  (5 shorter events, 0.0 us)
Async XLA Ops:
  7.2 112.6 %copy-start.2 = (f32[16]{0:T(128)S(1)}, f32[16]{0:T(128)}, u32[]{:S(2)}) copy-start(f32[16]{0:T(128)} %param.13) | copy-start | bytes 196
  7.2 112.6 %copy-start = (f32[16,4096]{1,0:T(8,128)S(1)}, f32[16,4096]{1,0:T(8,128)}, u32[]{:S(2)}) copy-start(f32[16,4096]{1,0:T(8,128)} %param.10) | copy-start | bytes 786436
  7.2 112.6 %copy-start.1 = (f32[16,16]{1,0:T(8,128)S(1)}, f32[16,16]{1,0:T(8,128)}, u32[]{:S(2)}) copy-start(f32[16,16]{1,0:T(8,128)} %param.9) | copy-start | bytes 3076
  7.2 389.8 %all-reduce.10.cloned.1.call-start = ((), (), s32[]{:S(2)}) async-start(), calls=%async_computation.1 | async-start | bytes 1048576 | tf_op jit(solution)/shard_map/psum | solution.py:32
  125.2 747.8 %all-reduce.8.cloned.1.call-start = ((), (), s32[]{:S(2)}) async-start(), calls=%async_computation | async-start | bytes 1048576 | tf_op jit(solution)/shard_map/psum | solution.py:32
Sparse Core Ops, SparseCore 0:
  125.3 271.6 all-reduce.9
  603.1 269.8 all-reduce.7
where the time goes:
time: 982 us; the launch traced here: 981 us
  waiting for transfers between devices  542 us (55%)
  blocking collectives  400 us (41%)
  other arithmetic  23.8 us (2%)
  between operations  14.8 us (2%)
    psum x2, waiting for transfers between devices, on_device(): site_num, site_den = lax.psum((site_num, site_den), 'ev')  542 us
    psum x2, blocking collectives, on_device(): absum, count = lax.psum((abs_part, count_part), ('ev', 'ch'))  202 us
    psum x2, blocking collectives, on_device(): lax.psum((jnp.sum(product, axis=2), jnp.sum(weight, axis=2)), 'ch')  198 us
  transfers between devices with their start and end apart: 2, of which 2 were waited for; matrix products, arithmetic and copies ran while one was open for 0% of the time, Pallas kernels for 0%

commit v1 on v0

--- a/solution.py
+++ b/solution.py
@@ -21,7 +21,7 @@
     for step in range(ITERS):
         resid = spectra - source[:, :, None] - site[None, :, :] + path
         abs_part = jnp.sum(valid * jnp.abs(resid), axis=(0, 2))
-        absum, count = lax.psum((abs_part, count_part), ("ev", "ch"))
+        absum, count = lax.psum(lax.psum((abs_part, count_part), "ev"), "ch")
         delta = 1.345 * (1.2533 * absum / jnp.maximum(count, 1.0) + 1e-05)
         limit = delta[None, :, None]
         weight = limit / jnp.maximum(jnp.abs(resid), limit) * valid

time: 982 us -> 1020 us (1.039)
  blocking collectives: 400 us -> 436 us
    psum x2 -> x4, blocking collectives: 202 us -> 239 us  [on_device(): absum, count = lax.psum(lax.psum((abs_part, count_part), 'ev'), 'ch')]
where the time goes in v1:
time: 1020 us
  waiting for transfers between devices  547 us (54%)
  blocking collectives  436 us (43%)
  other arithmetic  23.8 us (2%)
  between operations  14.8 us (1%)
    psum x2, waiting for transfers between devices, on_device(): site_num, site_den = lax.psum((site_num, site_den), 'ev')  547 us
    psum x4, blocking collectives, on_device(): absum, count = lax.psum(lax.psum((abs_part, count_part), 'ev'), 'ch')  239 us
    psum x2, blocking collectives, on_device(): lax.psum((jnp.sum(product, axis=2), jnp.sum(weight, axis=2)), 'ch')  198 us
  transfers between devices with their start and end apart: 2, of which 2 were waited for; matrix products, arithmetic and copies ran while one was open for 0% of the time, Pallas kernels for 0%

profile of v1, /device:TPU:8, one launch (start us, length us, event | category | flops | bytes accessed | tf_op | source)
XLA Modules:
  0.0 1023.1 jit_solution(6069354510742669470)
XLA Ops:
  7.2 0.0 copy-start.2
  7.2 0.0 copy-start
  7.2 0.0 copy-start.1
  7.2 0.0 all-reduce.11.cloned.1.call-start
  7.2 0.8 slice_bitcast_fusion.1
  8.0 0.7 convert_element_type.13
  8.7 0.7 broadcast_reduce_fusion
  9.5 0.9 fusion.8
  10.3 0.1 broadcast_in_dim.2
  10.5 0.2 copy.11
  10.6 0.2 sqrt_multiply_fusion
  10.8 3.4 multiply_reduce_fusion.1
  14.2 67.8 %all-reduce = (f32[16]{0:T(128)S(1)}, f32[]{:T(128)}) all-reduce(f32[16]{0:T(128)S(1)} %multiply_reduce_fusion.1, f32[]{:T(128)} %broadcast_reduce_fusion), channel_id=1, replica_groups=mesh['ev'=32,'ch'=16] {'ev'}, use_global_device_ids=true, to_apply=%region_1.0 | all-reduce | flops 17 | bytes 136 | tf_op jit(solution)/shard_map/psum | solution.py:24
  81.9 58.2 %all-reduce.5 = (f32[16]{0:T(128)S(1)}, f32[]{:T(128)}) all-reduce(f32[16]{0:T(128)S(1)} %get-tuple-element.10, f32[]{:T(128)} %get-tuple-element.11), channel_id=1, replica_groups=mesh['ev'=32,'ch'=16] {'ch'}, use_global_device_ids=true, to_apply=%region_2.0 | all-reduce | flops 17 | bytes 136 | tf_op jit(solution)/shard_map/psum | solution.py:24
  140.8 0.0 copy-done.2
  140.8 0.0 copy-done
  140.8 0.0 copy-done.1
  140.9 5.4 fusion.4
  146.2 0.0 all-reduce.11.cloned.1.call-update
  146.2 0.0 all-reduce.9.cloned.1.call-start
  146.3 273.8 %all-reduce.11.cloned.1.call-done = (f32[16,4096]{1,0:T(8,128)}, f32[16,4096]{1,0:T(8,128)}) async-done(((f32[16,4096]{1,0:T(8,128)}, f32[16,4096]{1,0:T(8,128)}), (f32[16,4096]{1,0:T(8,128)}, f32[16,4096]{1,0:T(8,128)})) %all-reduce.11.cloned.1.call-update) | async-done | bytes 524304 | tf_op jit(solution)/shard_map/psum | solution.py:32
  420.1 1.2 fusion.7
  421.3 98.8 %all-reduce.4 = (f32[16,16]{1,0:T(8,128)S(1)}, f32[16,16]{1,0:T(8,128)S(1)}, f32[16]{0:T(128)S(1)}) all-reduce(f32[16,16]{1,0:T(8,128)S(1)} %get-tuple-element.9, f32[16,16]{1,0:T(8,128)S(1)} %get-tuple-element.5, f32[16]{0:T(128)S(1)} %get-tuple-element.26), channel_id=1, replica_groups=mesh['ev'=32,'ch'=16] {'ch'}, use_global_device_ids=true, to_apply=%region_9.0 | all-reduce | flops 528 | bytes 4224 | tf_op jit(solution)/shard_map/psum | solution.py:29
  520.1 0.1 broadcast_subtract_fusion.1
  520.2 3.3 multiply_reduce_fusion
  523.5 66.6 %psum.127 = f32[16]{0:T(128)S(1)} all-reduce(f32[16]{0:T(128)S(1)} %multiply_reduce_fusion), channel_id=1, replica_groups=mesh['ev'=32,'ch'=16] {'ev'}, use_global_device_ids=true, to_apply=%region_17.0 | all-reduce | flops 16 | bytes 128 | tf_op jit(solution)/shard_map/psum | solution.py:24
  590.1 46.2 %psum.128 = f32[16]{0:T(128)S(1)} all-reduce(f32[16]{0:T(128)S(1)} %psum.127), channel_id=1, replica_groups=mesh['ev'=32,'ch'=16] {'ch'}, use_global_device_ids=true, to_apply=%region_18.0 | all-reduce | flops 16 | bytes 128 | tf_op jit(solution)/shard_map/psum | solution.py:24
  636.3 5.4 fusion.2
  641.7 0.0 all-reduce.9.cloned.1.call-update
  641.7 273.1 %all-reduce.9.cloned.1.call-done = (f32[16,4096]{1,0:T(8,128)}, f32[16,4096]{1,0:T(8,128)}) async-done(((f32[16,4096]{1,0:T(8,128)}, f32[16,4096]{1,0:T(8,128)}), (f32[16,4096]{1,0:T(8,128)}, f32[16,4096]{1,0:T(8,128)})) %all-reduce.9.cloned.1.call-update) | async-done | bytes 524304 | tf_op jit(solution)/shard_map/psum | solution.py:32
  914.8 1.2 fusion.6
  916.0 98.8 %all-reduce.3 = (f32[16,16]{1,0:T(8,128)S(1)}, f32[16,16]{1,0:T(8,128)S(1)}, f32[16]{0:T(128)S(1)}) all-reduce(f32[16,16]{1,0:T(8,128)S(1)} %get-tuple-element.7, f32[16,16]{1,0:T(8,128)S(1)} %get-tuple-element.3, f32[16]{0:T(128)S(1)} %get-tuple-element.24), channel_id=1, replica_groups=mesh['ev'=32,'ch'=16] {'ch'}, use_global_device_ids=true, to_apply=%region_22.0 | all-reduce | flops 528 | bytes 4224 | tf_op jit(solution)/shard_map/psum | solution.py:29
  1014.8 0.8 broadcast_subtract_fusion
  1015.6 0.6 add_add_fusion
  (5 shorter events, 0.0 us)
Async XLA Ops:
  7.2 133.7 %copy-start.2 = (f32[16]{0:T(128)S(1)}, f32[16]{0:T(128)}, u32[]{:S(2)}) copy-start(f32[16]{0:T(128)} %param.13) | copy-start | bytes 196
  7.2 133.7 %copy-start = (f32[16,4096]{1,0:T(8,128)S(1)}, f32[16,4096]{1,0:T(8,128)}, u32[]{:S(2)}) copy-start(f32[16,4096]{1,0:T(8,128)} %param.10) | copy-start | bytes 786436
  7.2 133.7 %copy-start.1 = (f32[16,16]{1,0:T(8,128)S(1)}, f32[16,16]{1,0:T(8,128)}, u32[]{:S(2)}) copy-start(f32[16,16]{1,0:T(8,128)} %param.9) | copy-start | bytes 3076
  7.2 412.9 %all-reduce.11.cloned.1.call-start = ((), (), s32[]{:S(2)}) async-start(), calls=%async_computation.1 | async-start | bytes 1048576 | tf_op jit(solution)/shard_map/psum | solution.py:32
  146.2 768.5 %all-reduce.9.cloned.1.call-start = ((), (), s32[]{:S(2)}) async-start(), calls=%async_computation | async-start | bytes 1048576 | tf_op jit(solution)/shard_map/psum | solution.py:32
Sparse Core Ops, SparseCore 0:
  146.4 273.6 all-reduce.10
  641.8 272.9 all-reduce.8
